TPU v7x, 512 devices: a whole 4x8x8 slice. The times are simulated.
512 devices in a mesh: wide: 64 (over y, z_lo, core), rep: 8 (over z_hi, x).
Axes of the slice: x: 4, y: 8, z: 8 (z_hi: 2, z_lo: 4; z = z_hi * 4 + z_lo), core: 2. Of those that a mesh axis runs over, the one named last changes fastest.
Arguments:
- features: bfloat16 [65536, 512], P(('wide', 'rep')), may hold values from -6 to 6
- w_query: bfloat16 [512, 512], replicated, may hold values from -0.25 to 0.25
- w_key: bfloat16 [512, 512], replicated, may hold values from -0.25 to 0.25
- w_out: bfloat16 [512, 512], replicated, may hold values from -0.25 to 0.25
- edge_weight: bfloat16 [64, 8, 96, 128, 128], P('wide', 'rep'), may hold values from -0.23925781 to 0.23925781
- tile_slot: int32 [64, 8, 96], P('wide', 'rep'), may hold values from 0 to 511, as said below
- tile_count: int32 [64, 8], P('wide', 'rep'), may hold values from 1 to 96, as said below
Outputs:
- updated: bfloat16 [65536, 512], P(('wide', 'rep'))
Inputs may be any that keep to these rules, and one draw needn't show every extreme that they name: For each w and r the first tile_count[w, r] entries of tile_slot[w, r] are distinct and ascending; all 96 entries of a list are distinct. `tile_count`: some device has 96 live tiles.
All inputs are finite; a program needn't handle non-finite values.
Results may differ from a plain program's by a relative error of at most 0.014.
Values may be sent and summed in bfloat16 or wider, within the bound.
A program may use at most 64 MiB of HBM per device.

v0:
```python
import jax
import jax.numpy as jnp
from jax import lax
from jax.sharding import PartitionSpec as P


def from_behind(block, axis, distance):
    devices = range(lax.axis_size(axis))
    route = [((i - distance) % len(devices), i) for i in devices]
    return lax.ppermute(block, axis, route)


def on_device(features, w_query, w_key, w_out, edge_weight, tile_slot, tile_count):
    tile_rows = features.shape[0]
    feat_width = features.shape[1]
    n_wide = lax.axis_size("wide")
    n_rep = lax.axis_size("rep")
    query_rows = jnp.dot(features, w_query, preferred_element_type=jnp.float32).astype(jnp.bfloat16)
    key_rows = jnp.dot(features, w_key, preferred_element_type=jnp.float32).astype(jnp.bfloat16)
    receivers = lax.all_gather(query_rows, "rep", axis=0, tiled=True)
    tile_slots = tile_slot[0, 0]
    live_count = tile_count[0, 0]
    weights = edge_weight[0, 0]
    step_of = tile_slots // n_rep
    active = jnp.arange(tile_slots.shape[0], dtype=jnp.int32) < live_count
    below = step_of[None, :] < jnp.arange(n_wide + 1, dtype=jnp.int32)[:, None]
    bounds = jnp.sum((active[None, :] & below).astype(jnp.int32), axis=1)
    factor = 1.0 / float(feat_width) ** 0.5

    def one_tile(tile_num, sender, partial_value):
        block = tile_slots[tile_num] % n_rep
        targets = lax.dynamic_slice_in_dim(receivers, block * tile_rows, tile_rows, 0)
        scores = (
            lax.dot_general(
                targets, sender, (((1,), (1,)), ((), ())), preferred_element_type=jnp.float32
            )
            * factor
        )
        weighted = (jnp.tanh(scores) * weights[tile_num].astype(jnp.float32)).astype(jnp.bfloat16)
        contrib = jnp.dot(weighted, sender, preferred_element_type=jnp.float32)
        previous = lax.dynamic_slice_in_dim(partial_value, block * tile_rows, tile_rows, 0)
        return lax.dynamic_update_slice_in_dim(
            partial_value, previous + contrib, block * tile_rows, 0
        )

    def one_step(step_num, sender, partial_value):
        return lax.fori_loop(
            bounds[step_num],
            bounds[step_num + 1],
            lambda tile_num, acc: one_tile(tile_num, sender, acc),
            partial_value,
        )

    partial_value = jnp.zeros((n_rep * tile_rows, feat_width), jnp.float32)
    partial_value = one_step(0, key_rows, partial_value)

    def advance(step_num, state_pair):
        sender = from_behind(state_pair[0], "wide", 1)
        return (sender, one_step(step_num, sender, state_pair[1]))

    partial_value = lax.fori_loop(1, n_wide, advance, (key_rows, partial_value))[1]
    summed = lax.psum_scatter(
        partial_value.astype(jnp.bfloat16), "rep", scatter_dimension=0, tiled=True
    )
    mixed = features.astype(jnp.float32) + jnp.dot(
        summed, w_out, preferred_element_type=jnp.float32
    )
    return mixed.astype(jnp.bfloat16)


def solution(mesh):
    in_specs = (
        P(("wide", "rep"), None),
        P(),
        P(),
        P(),
        P("wide", "rep", None, None, None),
        P("wide", "rep", None),
        P("wide", "rep"),
    )
    out_specs = P(("wide", "rep"), None)
    return jax.shard_map(
        on_device, mesh=mesh, in_specs=in_specs, out_specs=out_specs, check_vma=False
    )
```

profile of v0, /device:TPU:8, one launch (start us, length us, event | category | flops | bytes accessed | tf_op | source)
XLA Modules:
  0.0 2005.7 jit_solution(4528999640472336238)
XLA Ops:
  12.8 69.9 %all-gather.2.cloned.1.call-done = bf16[1024,512]{1,0:T(8,128)(2,1)} async-done(((bf16[128,512]{1,0:T(8,128)(2,1)}), bf16[1024,512]{1,0:T(8,128)(2,1)}) %all-gather.2.cloned.1.call-update) | async-done | bytes 1048592 | tf_op jit(solution)/shard_map/all_gather | solution.py:20
  92.7 1685.8 %while.66 = (s32[]{:T(128)}, bf16[128,512]{1,0:T(8,128)(2,1)S(1)}, f32[1024,512]{1,0:T(8,128)S(1)}, s32[65]{0:T(128)S(1)}, s32[96]{0:T(128)S(1)}, /*index=5*/bf1...) while((s32[]{:T(128)}, bf16[128,512]{1,0:T(8,128)(2,1)S(1)}, ...), condition=%wide.region_6.7_spmd, body=%wide.region_3.6_spmd.sunk | while | flops 33685532 | bytes 1739011 | solution.py:61
  177.3 26.8 %collective-permute-start = (bf16[128,512]{1,0:T(8,128)(2,1)S(1)}, bf16[128,512]{1,0:T(8,128)(2,1)S(1)}, u32[]{:S(2)}, u32[]{:S(2)}) collective-permute-start(bf16[128,512]{1,0:T(8,128)(2,1)S(1)} %get-tuple-element.784), channel_id=1, source_target_pairs={{504,0},{0,8},{8,16},{16,24},{24,32},{32,40},{40,48},{48,56},{56,6... | collective-permute-start | bytes 393224 | tf_op jit(solution)/shard_map/while/body/eval_jaxpr/ppermute | solution.py:10
  216.5 27.7 %collective-permute-start = (bf16[128,512]{1,0:T(8,128)(2,1)S(1)}, bf16[128,512]{1,0:T(8,128)(2,1)S(1)}, u32[]{:S(2)}, u32[]{:S(2)}) collective-permute-start(bf16[128,512]{1,0:T(8,128)(2,1)S(1)} %get-tuple-element.784), channel_id=1, source_target_pairs={{504,0},{0,8},{8,16},{16,24},{24,32},{32,40},{40,48},{48,56},{56,6... | collective-permute-start | bytes 393224 | tf_op jit(solution)/shard_map/while/body/eval_jaxpr/ppermute | solution.py:10
  368.7 22.0 %collective-permute-start = (bf16[128,512]{1,0:T(8,128)(2,1)S(1)}, bf16[128,512]{1,0:T(8,128)(2,1)S(1)}, u32[]{:S(2)}, u32[]{:S(2)}) collective-permute-start(bf16[128,512]{1,0:T(8,128)(2,1)S(1)} %get-tuple-element.784), channel_id=1, source_target_pairs={{504,0},{0,8},{8,16},{16,24},{24,32},{32,40},{40,48},{48,56},{56,6... | collective-permute-start | bytes 393224 | tf_op jit(solution)/shard_map/while/body/eval_jaxpr/ppermute | solution.py:10
  393.0 22.0 %collective-permute-start = (bf16[128,512]{1,0:T(8,128)(2,1)S(1)}, bf16[128,512]{1,0:T(8,128)(2,1)S(1)}, u32[]{:S(2)}, u32[]{:S(2)}) collective-permute-start(bf16[128,512]{1,0:T(8,128)(2,1)S(1)} %get-tuple-element.784), channel_id=1, source_target_pairs={{504,0},{0,8},{8,16},{16,24},{24,32},{32,40},{40,48},{48,56},{56,6... | collective-permute-start | bytes 393224 | tf_op jit(solution)/shard_map/while/body/eval_jaxpr/ppermute | solution.py:10
  453.3 40.4 %collective-permute-done = bf16[128,512]{1,0:T(8,128)(2,1)S(1)} collective-permute-done((bf16[128,512]{1,0:T(8,128)(2,1)S(1)}, bf16[128,512]{1,0:T(8,128)(2,1)S(1)}, u32[]{:S(2)}, u32[]{:S(2)}) %collective-permute-start) | collective-permute-done | bytes 131104 | tf_op jit(solution)/shard_map/while/body/eval_jaxpr/ppermute | solution.py:10
  497.6 28.8 %collective-permute-done = bf16[128,512]{1,0:T(8,128)(2,1)S(1)} collective-permute-done((bf16[128,512]{1,0:T(8,128)(2,1)S(1)}, bf16[128,512]{1,0:T(8,128)(2,1)S(1)}, u32[]{:S(2)}, u32[]{:S(2)}) %collective-permute-start) | collective-permute-done | bytes 131104 | tf_op jit(solution)/shard_map/while/body/eval_jaxpr/ppermute | solution.py:10
  546.0 37.2 %collective-permute-done = bf16[128,512]{1,0:T(8,128)(2,1)S(1)} collective-permute-done((bf16[128,512]{1,0:T(8,128)(2,1)S(1)}, bf16[128,512]{1,0:T(8,128)(2,1)S(1)}, u32[]{:S(2)}, u32[]{:S(2)}) %collective-permute-start) | collective-permute-done | bytes 131104 | tf_op jit(solution)/shard_map/while/body/eval_jaxpr/ppermute | solution.py:10
  658.6 22.0 %collective-permute-start = (bf16[128,512]{1,0:T(8,128)(2,1)S(1)}, bf16[128,512]{1,0:T(8,128)(2,1)S(1)}, u32[]{:S(2)}, u32[]{:S(2)}) collective-permute-start(bf16[128,512]{1,0:T(8,128)(2,1)S(1)} %get-tuple-element.784), channel_id=1, source_target_pairs={{504,0},{0,8},{8,16},{16,24},{24,32},{32,40},{40,48},{48,56},{56,6... | collective-permute-start | bytes 393224 | tf_op jit(solution)/shard_map/while/body/eval_jaxpr/ppermute | solution.py:10
  681.2 33.0 %collective-permute-done = bf16[128,512]{1,0:T(8,128)(2,1)S(1)} collective-permute-done((bf16[128,512]{1,0:T(8,128)(2,1)S(1)}, bf16[128,512]{1,0:T(8,128)(2,1)S(1)}, u32[]{:S(2)}, u32[]{:S(2)}) %collective-permute-start) | collective-permute-done | bytes 131104 | tf_op jit(solution)/shard_map/while/body/eval_jaxpr/ppermute | solution.py:10
  763.5 48.6 %collective-permute-done = bf16[128,512]{1,0:T(8,128)(2,1)S(1)} collective-permute-done((bf16[128,512]{1,0:T(8,128)(2,1)S(1)}, bf16[128,512]{1,0:T(8,128)(2,1)S(1)}, u32[]{:S(2)}, u32[]{:S(2)}) %collective-permute-start) | collective-permute-done | bytes 131104 | tf_op jit(solution)/shard_map/while/body/eval_jaxpr/ppermute | solution.py:10
  853.5 30.2 %collective-permute-done = bf16[128,512]{1,0:T(8,128)(2,1)S(1)} collective-permute-done((bf16[128,512]{1,0:T(8,128)(2,1)S(1)}, bf16[128,512]{1,0:T(8,128)(2,1)S(1)}, u32[]{:S(2)}, u32[]{:S(2)}) %collective-permute-start) | collective-permute-done | bytes 131104 | tf_op jit(solution)/shard_map/while/body/eval_jaxpr/ppermute | solution.py:10
  897.7 36.4 %collective-permute-done = bf16[128,512]{1,0:T(8,128)(2,1)S(1)} collective-permute-done((bf16[128,512]{1,0:T(8,128)(2,1)S(1)}, bf16[128,512]{1,0:T(8,128)(2,1)S(1)}, u32[]{:S(2)}, u32[]{:S(2)}) %collective-permute-start) | collective-permute-done | bytes 131104 | tf_op jit(solution)/shard_map/while/body/eval_jaxpr/ppermute | solution.py:10
  935.4 22.6 %collective-permute-start = (bf16[128,512]{1,0:T(8,128)(2,1)S(1)}, bf16[128,512]{1,0:T(8,128)(2,1)S(1)}, u32[]{:S(2)}, u32[]{:S(2)}) collective-permute-start(bf16[128,512]{1,0:T(8,128)(2,1)S(1)} %get-tuple-element.784), channel_id=1, source_target_pairs={{504,0},{0,8},{8,16},{16,24},{24,32},{32,40},{40,48},{48,56},{56,6... | collective-permute-start | bytes 393224 | tf_op jit(solution)/shard_map/while/body/eval_jaxpr/ppermute | solution.py:10
  963.7 45.6 %collective-permute-done = bf16[128,512]{1,0:T(8,128)(2,1)S(1)} collective-permute-done((bf16[128,512]{1,0:T(8,128)(2,1)S(1)}, bf16[128,512]{1,0:T(8,128)(2,1)S(1)}, u32[]{:S(2)}, u32[]{:S(2)}) %collective-permute-start) | collective-permute-done | bytes 131104 | tf_op jit(solution)/shard_map/while/body/eval_jaxpr/ppermute | solution.py:10
  1253.9 68.2 %collective-permute-done = bf16[128,512]{1,0:T(8,128)(2,1)S(1)} collective-permute-done((bf16[128,512]{1,0:T(8,128)(2,1)S(1)}, bf16[128,512]{1,0:T(8,128)(2,1)S(1)}, u32[]{:S(2)}, u32[]{:S(2)}) %collective-permute-start) | collective-permute-done | bytes 131104 | tf_op jit(solution)/shard_map/while/body/eval_jaxpr/ppermute | solution.py:10
  1441.4 21.4 %collective-permute-done = bf16[128,512]{1,0:T(8,128)(2,1)S(1)} collective-permute-done((bf16[128,512]{1,0:T(8,128)(2,1)S(1)}, bf16[128,512]{1,0:T(8,128)(2,1)S(1)}, u32[]{:S(2)}, u32[]{:S(2)}) %collective-permute-start) | collective-permute-done | bytes 131104 | tf_op jit(solution)/shard_map/while/body/eval_jaxpr/ppermute | solution.py:10
  1473.4 27.9 %collective-permute-done = bf16[128,512]{1,0:T(8,128)(2,1)S(1)} collective-permute-done((bf16[128,512]{1,0:T(8,128)(2,1)S(1)}, bf16[128,512]{1,0:T(8,128)(2,1)S(1)}, u32[]{:S(2)}, u32[]{:S(2)}) %collective-permute-start) | collective-permute-done | bytes 131104 | tf_op jit(solution)/shard_map/while/body/eval_jaxpr/ppermute | solution.py:10
  1513.5 32.7 %collective-permute-done = bf16[128,512]{1,0:T(8,128)(2,1)S(1)} collective-permute-done((bf16[128,512]{1,0:T(8,128)(2,1)S(1)}, bf16[128,512]{1,0:T(8,128)(2,1)S(1)}, u32[]{:S(2)}, u32[]{:S(2)}) %collective-permute-start) | collective-permute-done | bytes 131104 | tf_op jit(solution)/shard_map/while/body/eval_jaxpr/ppermute | solution.py:10
  1558.4 41.1 %collective-permute-done = bf16[128,512]{1,0:T(8,128)(2,1)S(1)} collective-permute-done((bf16[128,512]{1,0:T(8,128)(2,1)S(1)}, bf16[128,512]{1,0:T(8,128)(2,1)S(1)}, u32[]{:S(2)}, u32[]{:S(2)}) %collective-permute-start) | collective-permute-done | bytes 131104 | tf_op jit(solution)/shard_map/while/body/eval_jaxpr/ppermute | solution.py:10
  1645.3 42.3 %collective-permute-done = bf16[128,512]{1,0:T(8,128)(2,1)S(1)} collective-permute-done((bf16[128,512]{1,0:T(8,128)(2,1)S(1)}, bf16[128,512]{1,0:T(8,128)(2,1)S(1)}, u32[]{:S(2)}, u32[]{:S(2)}) %collective-permute-start) | collective-permute-done | bytes 131104 | tf_op jit(solution)/shard_map/while/body/eval_jaxpr/ppermute | solution.py:10
  1699.7 37.2 %collective-permute-done = bf16[128,512]{1,0:T(8,128)(2,1)S(1)} collective-permute-done((bf16[128,512]{1,0:T(8,128)(2,1)S(1)}, bf16[128,512]{1,0:T(8,128)(2,1)S(1)}, u32[]{:S(2)}, u32[]{:S(2)}) %collective-permute-start) | collective-permute-done | bytes 131104 | tf_op jit(solution)/shard_map/while/body/eval_jaxpr/ppermute | solution.py:10
  1779.7 217.4 %reduce-scatter.2.cloned.1.call-done = bf16[128,512]{1,0:T(8,128)(2,1)} async-done(((bf16[1024,512]{1,0:T(8,128)(2,1)}), bf16[128,512]{1,0:T(8,128)(2,1)}) %reduce-scatter.2.cloned.1.call-update) | async-done | bytes 131088 | tf_op jit(solution)/shard_map/reduce_scatter | solution.py:62
  (364 shorter events, 1034.0 us)
Async XLA Ops:
  6.5 76.2 %all-gather.2.cloned.1.call-start = ((), (), s32[]{:S(2)}) async-start(), calls=%async_computation.1 | async-start | bytes 1179648 | tf_op jit(solution)/shard_map/all_gather | solution.py:20
  9.4 1987.6 %reduce-scatter.2.cloned.1.call-start = ((), (), s32[]{:S(2)}) async-start(), calls=%async_computation.2 | async-start | bytes 1179648 | tf_op jit(solution)/shard_map/reduce_scatter | solution.py:62
  177.3 27.7 %collective-permute-start = (bf16[128,512]{1,0:T(8,128)(2,1)S(1)}, bf16[128,512]{1,0:T(8,128)(2,1)S(1)}, u32[]{:S(2)}, u32[]{:S(2)}) collective-permute-start(bf16[128,512]{1,0:T(8,128)(2,1)S(1)} %get-tuple-element.784), channel_id=1, source_target_pairs={{504,0},{0,8},{8,16},{16,24},{24,32},{32,40},{40,48},{48,56},{56,6... | collective-permute-start | bytes 393224 | tf_op jit(solution)/shard_map/while/body/eval_jaxpr/ppermute | solution.py:10
  216.5 28.6 %collective-permute-start = (bf16[128,512]{1,0:T(8,128)(2,1)S(1)}, bf16[128,512]{1,0:T(8,128)(2,1)S(1)}, u32[]{:S(2)}, u32[]{:S(2)}) collective-permute-start(bf16[128,512]{1,0:T(8,128)(2,1)S(1)} %get-tuple-element.784), channel_id=1, source_target_pairs={{504,0},{0,8},{8,16},{16,24},{24,32},{32,40},{40,48},{48,56},{56,6... | collective-permute-start | bytes 393224 | tf_op jit(solution)/shard_map/while/body/eval_jaxpr/ppermute | solution.py:10
  299.9 23.0 %collective-permute-start = (bf16[128,512]{1,0:T(8,128)(2,1)S(1)}, bf16[128,512]{1,0:T(8,128)(2,1)S(1)}, u32[]{:S(2)}, u32[]{:S(2)}) collective-permute-start(bf16[128,512]{1,0:T(8,128)(2,1)S(1)} %get-tuple-element.784), channel_id=1, source_target_pairs={{504,0},{0,8},{8,16},{16,24},{24,32},{32,40},{40,48},{48,56},{56,6... | collective-permute-start | bytes 393224 | tf_op jit(solution)/shard_map/while/body/eval_jaxpr/ppermute | solution.py:10
  393.0 27.8 %collective-permute-start = (bf16[128,512]{1,0:T(8,128)(2,1)S(1)}, bf16[128,512]{1,0:T(8,128)(2,1)S(1)}, u32[]{:S(2)}, u32[]{:S(2)}) collective-permute-start(bf16[128,512]{1,0:T(8,128)(2,1)S(1)} %get-tuple-element.784), channel_id=1, source_target_pairs={{504,0},{0,8},{8,16},{16,24},{24,32},{32,40},{40,48},{48,56},{56,6... | collective-permute-start | bytes 393224 | tf_op jit(solution)/shard_map/while/body/eval_jaxpr/ppermute | solution.py:10
  446.3 47.5 %collective-permute-start = (bf16[128,512]{1,0:T(8,128)(2,1)S(1)}, bf16[128,512]{1,0:T(8,128)(2,1)S(1)}, u32[]{:S(2)}, u32[]{:S(2)}) collective-permute-start(bf16[128,512]{1,0:T(8,128)(2,1)S(1)} %get-tuple-element.784), channel_id=1, source_target_pairs={{504,0},{0,8},{8,16},{16,24},{24,32},{32,40},{40,48},{48,56},{56,6... | collective-permute-start | bytes 393224 | tf_op jit(solution)/shard_map/while/body/eval_jaxpr/ppermute | solution.py:10
  495.0 31.3 %collective-permute-start = (bf16[128,512]{1,0:T(8,128)(2,1)S(1)}, bf16[128,512]{1,0:T(8,128)(2,1)S(1)}, u32[]{:S(2)}, u32[]{:S(2)}) collective-permute-start(bf16[128,512]{1,0:T(8,128)(2,1)S(1)} %get-tuple-element.784), channel_id=1, source_target_pairs={{504,0},{0,8},{8,16},{16,24},{24,32},{32,40},{40,48},{48,56},{56,6... | collective-permute-start | bytes 393224 | tf_op jit(solution)/shard_map/while/body/eval_jaxpr/ppermute | solution.py:10
  543.5 39.7 %collective-permute-start = (bf16[128,512]{1,0:T(8,128)(2,1)S(1)}, bf16[128,512]{1,0:T(8,128)(2,1)S(1)}, u32[]{:S(2)}, u32[]{:S(2)}) collective-permute-start(bf16[128,512]{1,0:T(8,128)(2,1)S(1)} %get-tuple-element.784), channel_id=1, source_target_pairs={{504,0},{0,8},{8,16},{16,24},{24,32},{32,40},{40,48},{48,56},{56,6... | collective-permute-start | bytes 393224 | tf_op jit(solution)/shard_map/while/body/eval_jaxpr/ppermute | solution.py:10
  658.6 55.6 %collective-permute-start = (bf16[128,512]{1,0:T(8,128)(2,1)S(1)}, bf16[128,512]{1,0:T(8,128)(2,1)S(1)}, u32[]{:S(2)}, u32[]{:S(2)}) collective-permute-start(bf16[128,512]{1,0:T(8,128)(2,1)S(1)} %get-tuple-element.784), channel_id=1, source_target_pairs={{504,0},{0,8},{8,16},{16,24},{24,32},{32,40},{40,48},{48,56},{56,6... | collective-permute-start | bytes 393224 | tf_op jit(solution)/shard_map/while/body/eval_jaxpr/ppermute | solution.py:10
  755.6 56.4 %collective-permute-start = (bf16[128,512]{1,0:T(8,128)(2,1)S(1)}, bf16[128,512]{1,0:T(8,128)(2,1)S(1)}, u32[]{:S(2)}, u32[]{:S(2)}) collective-permute-start(bf16[128,512]{1,0:T(8,128)(2,1)S(1)} %get-tuple-element.784), channel_id=1, source_target_pairs={{504,0},{0,8},{8,16},{16,24},{24,32},{32,40},{40,48},{48,56},{56,6... | collective-permute-start | bytes 393224 | tf_op jit(solution)/shard_map/while/body/eval_jaxpr/ppermute | solution.py:10
  851.0 32.7 %collective-permute-start = (bf16[128,512]{1,0:T(8,128)(2,1)S(1)}, bf16[128,512]{1,0:T(8,128)(2,1)S(1)}, u32[]{:S(2)}, u32[]{:S(2)}) collective-permute-start(bf16[128,512]{1,0:T(8,128)(2,1)S(1)} %get-tuple-element.784), channel_id=1, source_target_pairs={{504,0},{0,8},{8,16},{16,24},{24,32},{32,40},{40,48},{48,56},{56,6... | collective-permute-start | bytes 393224 | tf_op jit(solution)/shard_map/while/body/eval_jaxpr/ppermute | solution.py:10
  895.2 38.9 %collective-permute-start = (bf16[128,512]{1,0:T(8,128)(2,1)S(1)}, bf16[128,512]{1,0:T(8,128)(2,1)S(1)}, u32[]{:S(2)}, u32[]{:S(2)}) collective-permute-start(bf16[128,512]{1,0:T(8,128)(2,1)S(1)} %get-tuple-element.784), channel_id=1, source_target_pairs={{504,0},{0,8},{8,16},{16,24},{24,32},{32,40},{40,48},{48,56},{56,6... | collective-permute-start | bytes 393224 | tf_op jit(solution)/shard_map/while/body/eval_jaxpr/ppermute | solution.py:10
  935.4 23.5 %collective-permute-start = (bf16[128,512]{1,0:T(8,128)(2,1)S(1)}, bf16[128,512]{1,0:T(8,128)(2,1)S(1)}, u32[]{:S(2)}, u32[]{:S(2)}) collective-permute-start(bf16[128,512]{1,0:T(8,128)(2,1)S(1)} %get-tuple-element.784), channel_id=1, source_target_pairs={{504,0},{0,8},{8,16},{16,24},{24,32},{32,40},{40,48},{48,56},{56,6... | collective-permute-start | bytes 393224 | tf_op jit(solution)/shard_map/while/body/eval_jaxpr/ppermute | solution.py:10
  960.2 49.1 %collective-permute-start = (bf16[128,512]{1,0:T(8,128)(2,1)S(1)}, bf16[128,512]{1,0:T(8,128)(2,1)S(1)}, u32[]{:S(2)}, u32[]{:S(2)}) collective-permute-start(bf16[128,512]{1,0:T(8,128)(2,1)S(1)} %get-tuple-element.784), channel_id=1, source_target_pairs={{504,0},{0,8},{8,16},{16,24},{24,32},{32,40},{40,48},{48,56},{56,6... | collective-permute-start | bytes 393224 | tf_op jit(solution)/shard_map/while/body/eval_jaxpr/ppermute | solution.py:10
  1010.5 23.0 %collective-permute-start = (bf16[128,512]{1,0:T(8,128)(2,1)S(1)}, bf16[128,512]{1,0:T(8,128)(2,1)S(1)}, u32[]{:S(2)}, u32[]{:S(2)}) collective-permute-start(bf16[128,512]{1,0:T(8,128)(2,1)S(1)} %get-tuple-element.784), channel_id=1, source_target_pairs={{504,0},{0,8},{8,16},{16,24},{24,32},{32,40},{40,48},{48,56},{56,6... | collective-permute-start | bytes 393224 | tf_op jit(solution)/shard_map/while/body/eval_jaxpr/ppermute | solution.py:10
  1168.4 28.9 %collective-permute-start = (bf16[128,512]{1,0:T(8,128)(2,1)S(1)}, bf16[128,512]{1,0:T(8,128)(2,1)S(1)}, u32[]{:S(2)}, u32[]{:S(2)}) collective-permute-start(bf16[128,512]{1,0:T(8,128)(2,1)S(1)} %get-tuple-element.784), channel_id=1, source_target_pairs={{504,0},{0,8},{8,16},{16,24},{24,32},{32,40},{40,48},{48,56},{56,6... | collective-permute-start | bytes 393224 | tf_op jit(solution)/shard_map/while/body/eval_jaxpr/ppermute | solution.py:10
  1251.4 70.7 %collective-permute-start = (bf16[128,512]{1,0:T(8,128)(2,1)S(1)}, bf16[128,512]{1,0:T(8,128)(2,1)S(1)}, u32[]{:S(2)}, u32[]{:S(2)}) collective-permute-start(bf16[128,512]{1,0:T(8,128)(2,1)S(1)} %get-tuple-element.784), channel_id=1, source_target_pairs={{504,0},{0,8},{8,16},{16,24},{24,32},{32,40},{40,48},{48,56},{56,6... | collective-permute-start | bytes 393224 | tf_op jit(solution)/shard_map/while/body/eval_jaxpr/ppermute | solution.py:10
  1438.9 23.9 %collective-permute-start = (bf16[128,512]{1,0:T(8,128)(2,1)S(1)}, bf16[128,512]{1,0:T(8,128)(2,1)S(1)}, u32[]{:S(2)}, u32[]{:S(2)}) collective-permute-start(bf16[128,512]{1,0:T(8,128)(2,1)S(1)} %get-tuple-element.784), channel_id=1, source_target_pairs={{504,0},{0,8},{8,16},{16,24},{24,32},{32,40},{40,48},{48,56},{56,6... | collective-permute-start | bytes 393224 | tf_op jit(solution)/shard_map/while/body/eval_jaxpr/ppermute | solution.py:10
  1464.1 37.3 %collective-permute-start = (bf16[128,512]{1,0:T(8,128)(2,1)S(1)}, bf16[128,512]{1,0:T(8,128)(2,1)S(1)}, u32[]{:S(2)}, u32[]{:S(2)}) collective-permute-start(bf16[128,512]{1,0:T(8,128)(2,1)S(1)} %get-tuple-element.784), channel_id=1, source_target_pairs={{504,0},{0,8},{8,16},{16,24},{24,32},{32,40},{40,48},{48,56},{56,6... | collective-permute-start | bytes 393224 | tf_op jit(solution)/shard_map/while/body/eval_jaxpr/ppermute | solution.py:10
  1511.0 35.3 %collective-permute-start = (bf16[128,512]{1,0:T(8,128)(2,1)S(1)}, bf16[128,512]{1,0:T(8,128)(2,1)S(1)}, u32[]{:S(2)}, u32[]{:S(2)}) collective-permute-start(bf16[128,512]{1,0:T(8,128)(2,1)S(1)} %get-tuple-element.784), channel_id=1, source_target_pairs={{504,0},{0,8},{8,16},{16,24},{24,32},{32,40},{40,48},{48,56},{56,6... | collective-permute-start | bytes 393224 | tf_op jit(solution)/shard_map/while/body/eval_jaxpr/ppermute | solution.py:10
  1555.8 43.6 %collective-permute-start = (bf16[128,512]{1,0:T(8,128)(2,1)S(1)}, bf16[128,512]{1,0:T(8,128)(2,1)S(1)}, u32[]{:S(2)}, u32[]{:S(2)}) collective-permute-start(bf16[128,512]{1,0:T(8,128)(2,1)S(1)} %get-tuple-element.784), channel_id=1, source_target_pairs={{504,0},{0,8},{8,16},{16,24},{24,32},{32,40},{40,48},{48,56},{56,6... | collective-permute-start | bytes 393224 | tf_op jit(solution)/shard_map/while/body/eval_jaxpr/ppermute | solution.py:10
  1642.7 44.8 %collective-permute-start = (bf16[128,512]{1,0:T(8,128)(2,1)S(1)}, bf16[128,512]{1,0:T(8,128)(2,1)S(1)}, u32[]{:S(2)}, u32[]{:S(2)}) collective-permute-start(bf16[128,512]{1,0:T(8,128)(2,1)S(1)} %get-tuple-element.784), channel_id=1, source_target_pairs={{504,0},{0,8},{8,16},{16,24},{24,32},{32,40},{40,48},{48,56},{56,6... | collective-permute-start | bytes 393224 | tf_op jit(solution)/shard_map/while/body/eval_jaxpr/ppermute | solution.py:10
  1697.2 39.7 %collective-permute-start = (bf16[128,512]{1,0:T(8,128)(2,1)S(1)}, bf16[128,512]{1,0:T(8,128)(2,1)S(1)}, u32[]{:S(2)}, u32[]{:S(2)}) collective-permute-start(bf16[128,512]{1,0:T(8,128)(2,1)S(1)} %get-tuple-element.784), channel_id=1, source_target_pairs={{504,0},{0,8},{8,16},{16,24},{24,32},{32,40},{40,48},{48,56},{56,6... | collective-permute-start | bytes 393224 | tf_op jit(solution)/shard_map/while/body/eval_jaxpr/ppermute | solution.py:10
  (45 other events, 1100.0 us)
Sparse Core Ops, SparseCore 0:
  10.5 72.1 all-gather.1
  1779.8 217.1 reduce-scatter.1
where the time goes:
time: 2020 us; the launch traced here: 2010 us
  waiting for transfers between devices  1270 us (63%)
  starting transfers between devices  392 us (19%)
  loops' own time  235 us (12%)
  local copies, waits for them, and re-layouts  55.7 us (3%)
  matrix products  35.8 us (2%)
    ppermute x63, waiting for transfers between devices, from_behind(): return lax.ppermute(block, axis, route)  984 us
    ppermute x63, starting transfers between devices, from_behind(): return lax.ppermute(block, axis, route)  392 us
    another operation x64, loops' own time, one_step(): lax.fori_loop(bounds[step_num], bounds[step_num + 1], lambda tile_num, ac...  232 us
    reduce_scatter x1, waiting for transfers between devices, on_device(): lax.psum_scatter(partial_value.astype(jnp.bfloat16), 'rep', scatter_dimen...  217 us
    all_gather x1, waiting for transfers between devices, on_device(): receivers = lax.all_gather(query_rows, 'rep', axis=0, tiled=True)  69.9 us
  transfers between devices with their start and end apart: 65, of which 65 were waited for; matrix products, arithmetic and copies ran while one was open for 2% of the time, Pallas kernels for 0%

commit v1 on v0

--- a/solution.py
+++ b/solution.py
@@ -2,6 +2,7 @@
 import jax.numpy as jnp
 from jax import lax
 from jax.sharding import PartitionSpec as P
+from jax.lax import all_to_all, axis_size
 
 
 def from_behind(block, axis, distance):
@@ -17,7 +18,13 @@
     n_rep = lax.axis_size("rep")
     query_rows = jnp.dot(features, w_query, preferred_element_type=jnp.float32).astype(jnp.bfloat16)
     key_rows = jnp.dot(features, w_key, preferred_element_type=jnp.float32).astype(jnp.bfloat16)
-    receivers = lax.all_gather(query_rows, "rep", axis=0, tiled=True)
+
+    def _use_slot(frame_in):
+        outcome_arr = axis_size("rep")
+        met_up = jnp.stack([frame_in] * outcome_arr)
+        return jnp.concatenate(all_to_all(met_up, "rep", 0, 0), axis=0)
+
+    receivers = _use_slot(query_rows)
     tile_slots = tile_slot[0, 0]
     live_count = tile_count[0, 0]
     weights = edge_weight[0, 0]

time: 2020 us -> 1910 us (0.946)
  waiting for transfers between devices: 1270 us -> 1180 us
    all_gather x1 -> x0, waiting for transfers between devices: 69.9 us -> none  [on_device(): receivers = lax.all_gather(query_rows, 'rep', axis=0, tiled=True)]
    ppermute x63, waiting for transfers between devices: 984 us -> 940 us  [from_behind(): return lax.ppermute(block, axis, route)]
    all_to_all x0 -> x1, waiting for transfers between devices: none -> 27.1 us  [_use_slot(): return jnp.concatenate(all_to_all(met_up, 'rep', 0, 0), axis=0)]
where the time goes in v1:
time: 1910 us; the launch traced here: 1900 us
  waiting for transfers between devices  1180 us (62%)
  starting transfers between devices  399 us (21%)
  loops' own time  220 us (12%)
  local copies, waits for them, and re-layouts  57.6 us (3%)
  matrix products  34 us (2%)
    ppermute x63, waiting for transfers between devices, from_behind(): return lax.ppermute(block, axis, route)  940 us
    ppermute x63, starting transfers between devices, from_behind(): return lax.ppermute(block, axis, route)  386 us
    another operation x64, loops' own time, one_step(): lax.fori_loop(bounds[step_num], bounds[step_num + 1], lambda tile_num, ac...  217 us
    reduce_scatter x1, waiting for transfers between devices, on_device(): lax.psum_scatter(partial_value.astype(jnp.bfloat16), 'rep', scatter_dimen...  208 us
  transfers between devices with their start and end apart: 65, of which 65 were waited for; matrix products, arithmetic and copies ran while one was open for 2% of the time, Pallas kernels for 0%

profile of v1, /device:TPU:8, one launch (start us, length us, event | category | flops | bytes accessed | tf_op | source)
XLA Modules:
  0.0 1901.5 jit_solution(972846846424928354)
XLA Ops:
  24.2 27.1 %all-to-all-done = bf16[8,128,512]{2,1,0:T(8,128)(2,1)S(1)} async-done(((bf16[8,128,512]{2,1,0:T(8,128)(2,1)}), bf16[8,128,512]{2,1,0:T(8,128)(2,1)S(1)}, u32[]{:S(2)}, u32[]{:S(2)}) %all-to-all-start) | async-done | bytes 1048608 | tf_op jit(solution)/shard_map/all_to_all | solution.py:25
  62.0 1621.3 %while.66 = (s32[]{:T(128)}, bf16[128,512]{1,0:T(8,128)(2,1)S(1)}, f32[1024,512]{1,0:T(8,128)S(1)}, s32[65]{0:T(128)S(1)}, s32[96]{0:T(128)S(1)}, /*index=5*/bf1...) while((s32[]{:T(128)}, bf16[128,512]{1,0:T(8,128)(2,1)S(1)}, ...), condition=%wide.region_6.7_spmd, body=%wide.region_3.6_spmd.sunk | while | flops 33685532 | bytes 1739011 | solution.py:68
  144.0 26.9 %collective-permute-start = (bf16[128,512]{1,0:T(8,128)(2,1)S(1)}, bf16[128,512]{1,0:T(8,128)(2,1)S(1)}, u32[]{:S(2)}, u32[]{:S(2)}) collective-permute-start(bf16[128,512]{1,0:T(8,128)(2,1)S(1)} %get-tuple-element.784), channel_id=1, source_target_pairs={{504,0},{0,8},{8,16},{16,24},{24,32},{32,40},{40,48},{48,56},{56,6... | collective-permute-start | bytes 393224 | tf_op jit(solution)/shard_map/while/body/eval_jaxpr/ppermute | solution.py:11
  183.2 26.5 %collective-permute-start = (bf16[128,512]{1,0:T(8,128)(2,1)S(1)}, bf16[128,512]{1,0:T(8,128)(2,1)S(1)}, u32[]{:S(2)}, u32[]{:S(2)}) collective-permute-start(bf16[128,512]{1,0:T(8,128)(2,1)S(1)} %get-tuple-element.784), channel_id=1, source_target_pairs={{504,0},{0,8},{8,16},{16,24},{24,32},{32,40},{40,48},{48,56},{56,6... | collective-permute-start | bytes 393224 | tf_op jit(solution)/shard_map/while/body/eval_jaxpr/ppermute | solution.py:11
  329.7 21.2 %collective-permute-start = (bf16[128,512]{1,0:T(8,128)(2,1)S(1)}, bf16[128,512]{1,0:T(8,128)(2,1)S(1)}, u32[]{:S(2)}, u32[]{:S(2)}) collective-permute-start(bf16[128,512]{1,0:T(8,128)(2,1)S(1)} %get-tuple-element.784), channel_id=1, source_target_pairs={{504,0},{0,8},{8,16},{16,24},{24,32},{32,40},{40,48},{48,56},{56,6... | collective-permute-start | bytes 393224 | tf_op jit(solution)/shard_map/while/body/eval_jaxpr/ppermute | solution.py:11
  353.0 21.2 %collective-permute-start = (bf16[128,512]{1,0:T(8,128)(2,1)S(1)}, bf16[128,512]{1,0:T(8,128)(2,1)S(1)}, u32[]{:S(2)}, u32[]{:S(2)}) collective-permute-start(bf16[128,512]{1,0:T(8,128)(2,1)S(1)} %get-tuple-element.784), channel_id=1, source_target_pairs={{504,0},{0,8},{8,16},{16,24},{24,32},{32,40},{40,48},{48,56},{56,6... | collective-permute-start | bytes 393224 | tf_op jit(solution)/shard_map/while/body/eval_jaxpr/ppermute | solution.py:11
  411.2 37.8 %collective-permute-done = bf16[128,512]{1,0:T(8,128)(2,1)S(1)} collective-permute-done((bf16[128,512]{1,0:T(8,128)(2,1)S(1)}, bf16[128,512]{1,0:T(8,128)(2,1)S(1)}, u32[]{:S(2)}, u32[]{:S(2)}) %collective-permute-start) | collective-permute-done | bytes 131104 | tf_op jit(solution)/shard_map/while/body/eval_jaxpr/ppermute | solution.py:11
  452.7 27.6 %collective-permute-done = bf16[128,512]{1,0:T(8,128)(2,1)S(1)} collective-permute-done((bf16[128,512]{1,0:T(8,128)(2,1)S(1)}, bf16[128,512]{1,0:T(8,128)(2,1)S(1)}, u32[]{:S(2)}, u32[]{:S(2)}) %collective-permute-start) | collective-permute-done | bytes 131104 | tf_op jit(solution)/shard_map/while/body/eval_jaxpr/ppermute | solution.py:11
  499.4 35.6 %collective-permute-done = bf16[128,512]{1,0:T(8,128)(2,1)S(1)} collective-permute-done((bf16[128,512]{1,0:T(8,128)(2,1)S(1)}, bf16[128,512]{1,0:T(8,128)(2,1)S(1)}, u32[]{:S(2)}, u32[]{:S(2)}) %collective-permute-start) | collective-permute-done | bytes 131104 | tf_op jit(solution)/shard_map/while/body/eval_jaxpr/ppermute | solution.py:11
  606.8 22.0 %collective-permute-start = (bf16[128,512]{1,0:T(8,128)(2,1)S(1)}, bf16[128,512]{1,0:T(8,128)(2,1)S(1)}, u32[]{:S(2)}, u32[]{:S(2)}) collective-permute-start(bf16[128,512]{1,0:T(8,128)(2,1)S(1)} %get-tuple-element.784), channel_id=1, source_target_pairs={{504,0},{0,8},{8,16},{16,24},{24,32},{32,40},{40,48},{48,56},{56,6... | collective-permute-start | bytes 393224 | tf_op jit(solution)/shard_map/while/body/eval_jaxpr/ppermute | solution.py:11
  629.4 30.2 %collective-permute-done = bf16[128,512]{1,0:T(8,128)(2,1)S(1)} collective-permute-done((bf16[128,512]{1,0:T(8,128)(2,1)S(1)}, bf16[128,512]{1,0:T(8,128)(2,1)S(1)}, u32[]{:S(2)}, u32[]{:S(2)}) %collective-permute-start) | collective-permute-done | bytes 131104 | tf_op jit(solution)/shard_map/while/body/eval_jaxpr/ppermute | solution.py:11
  707.0 46.5 %collective-permute-done = bf16[128,512]{1,0:T(8,128)(2,1)S(1)} collective-permute-done((bf16[128,512]{1,0:T(8,128)(2,1)S(1)}, bf16[128,512]{1,0:T(8,128)(2,1)S(1)}, u32[]{:S(2)}, u32[]{:S(2)}) %collective-permute-start) | collective-permute-done | bytes 131104 | tf_op jit(solution)/shard_map/while/body/eval_jaxpr/ppermute | solution.py:11
  793.6 29.0 %collective-permute-done = bf16[128,512]{1,0:T(8,128)(2,1)S(1)} collective-permute-done((bf16[128,512]{1,0:T(8,128)(2,1)S(1)}, bf16[128,512]{1,0:T(8,128)(2,1)S(1)}, u32[]{:S(2)}, u32[]{:S(2)}) %collective-permute-start) | collective-permute-done | bytes 131104 | tf_op jit(solution)/shard_map/while/body/eval_jaxpr/ppermute | solution.py:11
  836.4 34.4 %collective-permute-done = bf16[128,512]{1,0:T(8,128)(2,1)S(1)} collective-permute-done((bf16[128,512]{1,0:T(8,128)(2,1)S(1)}, bf16[128,512]{1,0:T(8,128)(2,1)S(1)}, u32[]{:S(2)}, u32[]{:S(2)}) %collective-permute-start) | collective-permute-done | bytes 131104 | tf_op jit(solution)/shard_map/while/body/eval_jaxpr/ppermute | solution.py:11
  872.0 21.4 %collective-permute-start = (bf16[128,512]{1,0:T(8,128)(2,1)S(1)}, bf16[128,512]{1,0:T(8,128)(2,1)S(1)}, u32[]{:S(2)}, u32[]{:S(2)}) collective-permute-start(bf16[128,512]{1,0:T(8,128)(2,1)S(1)} %get-tuple-element.784), channel_id=1, source_target_pairs={{504,0},{0,8},{8,16},{16,24},{24,32},{32,40},{40,48},{48,56},{56,6... | collective-permute-start | bytes 393224 | tf_op jit(solution)/shard_map/while/body/eval_jaxpr/ppermute | solution.py:11
  899.0 44.0 %collective-permute-done = bf16[128,512]{1,0:T(8,128)(2,1)S(1)} collective-permute-done((bf16[128,512]{1,0:T(8,128)(2,1)S(1)}, bf16[128,512]{1,0:T(8,128)(2,1)S(1)}, u32[]{:S(2)}, u32[]{:S(2)}) %collective-permute-start) | collective-permute-done | bytes 131104 | tf_op jit(solution)/shard_map/while/body/eval_jaxpr/ppermute | solution.py:11
  1178.3 64.9 %collective-permute-done = bf16[128,512]{1,0:T(8,128)(2,1)S(1)} collective-permute-done((bf16[128,512]{1,0:T(8,128)(2,1)S(1)}, bf16[128,512]{1,0:T(8,128)(2,1)S(1)}, u32[]{:S(2)}, u32[]{:S(2)}) %collective-permute-start) | collective-permute-done | bytes 131104 | tf_op jit(solution)/shard_map/while/body/eval_jaxpr/ppermute | solution.py:11
  1358.4 21.7 %collective-permute-done = bf16[128,512]{1,0:T(8,128)(2,1)S(1)} collective-permute-done((bf16[128,512]{1,0:T(8,128)(2,1)S(1)}, bf16[128,512]{1,0:T(8,128)(2,1)S(1)}, u32[]{:S(2)}, u32[]{:S(2)}) %collective-permute-start) | collective-permute-done | bytes 131104 | tf_op jit(solution)/shard_map/while/body/eval_jaxpr/ppermute | solution.py:11
  1389.1 27.8 %collective-permute-done = bf16[128,512]{1,0:T(8,128)(2,1)S(1)} collective-permute-done((bf16[128,512]{1,0:T(8,128)(2,1)S(1)}, bf16[128,512]{1,0:T(8,128)(2,1)S(1)}, u32[]{:S(2)}, u32[]{:S(2)}) %collective-permute-start) | collective-permute-done | bytes 131104 | tf_op jit(solution)/shard_map/while/body/eval_jaxpr/ppermute | solution.py:11
  1428.6 31.5 %collective-permute-done = bf16[128,512]{1,0:T(8,128)(2,1)S(1)} collective-permute-done((bf16[128,512]{1,0:T(8,128)(2,1)S(1)}, bf16[128,512]{1,0:T(8,128)(2,1)S(1)}, u32[]{:S(2)}, u32[]{:S(2)}) %collective-permute-start) | collective-permute-done | bytes 131104 | tf_op jit(solution)/shard_map/while/body/eval_jaxpr/ppermute | solution.py:11
  1471.8 39.5 %collective-permute-done = bf16[128,512]{1,0:T(8,128)(2,1)S(1)} collective-permute-done((bf16[128,512]{1,0:T(8,128)(2,1)S(1)}, bf16[128,512]{1,0:T(8,128)(2,1)S(1)}, u32[]{:S(2)}, u32[]{:S(2)}) %collective-permute-start) | collective-permute-done | bytes 131104 | tf_op jit(solution)/shard_map/while/body/eval_jaxpr/ppermute | solution.py:11
  1555.9 39.9 %collective-permute-done = bf16[128,512]{1,0:T(8,128)(2,1)S(1)} collective-permute-done((bf16[128,512]{1,0:T(8,128)(2,1)S(1)}, bf16[128,512]{1,0:T(8,128)(2,1)S(1)}, u32[]{:S(2)}, u32[]{:S(2)}) %collective-permute-start) | collective-permute-done | bytes 131104 | tf_op jit(solution)/shard_map/while/body/eval_jaxpr/ppermute | solution.py:11
  1607.5 35.6 %collective-permute-done = bf16[128,512]{1,0:T(8,128)(2,1)S(1)} collective-permute-done((bf16[128,512]{1,0:T(8,128)(2,1)S(1)}, bf16[128,512]{1,0:T(8,128)(2,1)S(1)}, u32[]{:S(2)}, u32[]{:S(2)}) %collective-permute-start) | collective-permute-done | bytes 131104 | tf_op jit(solution)/shard_map/while/body/eval_jaxpr/ppermute | solution.py:11
  1684.4 208.5 %reduce-scatter.2.cloned.1.call-done = bf16[128,512]{1,0:T(8,128)(2,1)} async-done(((bf16[1024,512]{1,0:T(8,128)(2,1)}), bf16[128,512]{1,0:T(8,128)(2,1)}) %reduce-scatter.2.cloned.1.call-update) | async-done | bytes 131088 | tf_op jit(solution)/shard_map/reduce_scatter | solution.py:69
  (368 shorter events, 1010.5 us)
Async XLA Ops:
  9.8 41.5 %all-to-all-start = ((bf16[8,128,512]{2,1,0:T(8,128)(2,1)}), bf16[8,128,512]{2,1,0:T(8,128)(2,1)S(1)}, u32[]{:S(2)}, u32[]{:S(2)}) async-start(bf16[8,128,512]{2,1,0:T(8,128)(2,1)} %stack.2), calls=%async_computation | async-start | bytes 2097152 | tf_op jit(solution)/shard_map/all_to_all | solution.py:25
  22.5 1870.3 %reduce-scatter.2.cloned.1.call-start = ((), (), s32[]{:S(2)}) async-start(), calls=%async_computation.2 | async-start | bytes 1179648 | tf_op jit(solution)/shard_map/reduce_scatter | solution.py:69
  144.0 27.9 %collective-permute-start = (bf16[128,512]{1,0:T(8,128)(2,1)S(1)}, bf16[128,512]{1,0:T(8,128)(2,1)S(1)}, u32[]{:S(2)}, u32[]{:S(2)}) collective-permute-start(bf16[128,512]{1,0:T(8,128)(2,1)S(1)} %get-tuple-element.784), channel_id=1, source_target_pairs={{504,0},{0,8},{8,16},{16,24},{24,32},{32,40},{40,48},{48,56},{56,6... | collective-permute-start | bytes 393224 | tf_op jit(solution)/shard_map/while/body/eval_jaxpr/ppermute | solution.py:11
  183.2 27.4 %collective-permute-start = (bf16[128,512]{1,0:T(8,128)(2,1)S(1)}, bf16[128,512]{1,0:T(8,128)(2,1)S(1)}, u32[]{:S(2)}, u32[]{:S(2)}) collective-permute-start(bf16[128,512]{1,0:T(8,128)(2,1)S(1)} %get-tuple-element.784), channel_id=1, source_target_pairs={{504,0},{0,8},{8,16},{16,24},{24,32},{32,40},{40,48},{48,56},{56,6... | collective-permute-start | bytes 393224 | tf_op jit(solution)/shard_map/while/body/eval_jaxpr/ppermute | solution.py:11
  262.1 22.2 %collective-permute-start = (bf16[128,512]{1,0:T(8,128)(2,1)S(1)}, bf16[128,512]{1,0:T(8,128)(2,1)S(1)}, u32[]{:S(2)}, u32[]{:S(2)}) collective-permute-start(bf16[128,512]{1,0:T(8,128)(2,1)S(1)} %get-tuple-element.784), channel_id=1, source_target_pairs={{504,0},{0,8},{8,16},{16,24},{24,32},{32,40},{40,48},{48,56},{56,6... | collective-permute-start | bytes 393224 | tf_op jit(solution)/shard_map/while/body/eval_jaxpr/ppermute | solution.py:11
  353.0 25.5 %collective-permute-start = (bf16[128,512]{1,0:T(8,128)(2,1)S(1)}, bf16[128,512]{1,0:T(8,128)(2,1)S(1)}, u32[]{:S(2)}, u32[]{:S(2)}) collective-permute-start(bf16[128,512]{1,0:T(8,128)(2,1)S(1)} %get-tuple-element.784), channel_id=1, source_target_pairs={{504,0},{0,8},{8,16},{16,24},{24,32},{32,40},{40,48},{48,56},{56,6... | collective-permute-start | bytes 393224 | tf_op jit(solution)/shard_map/while/body/eval_jaxpr/ppermute | solution.py:11
  403.1 45.9 %collective-permute-start = (bf16[128,512]{1,0:T(8,128)(2,1)S(1)}, bf16[128,512]{1,0:T(8,128)(2,1)S(1)}, u32[]{:S(2)}, u32[]{:S(2)}) collective-permute-start(bf16[128,512]{1,0:T(8,128)(2,1)S(1)} %get-tuple-element.784), channel_id=1, source_target_pairs={{504,0},{0,8},{8,16},{16,24},{24,32},{32,40},{40,48},{48,56},{56,6... | collective-permute-start | bytes 393224 | tf_op jit(solution)/shard_map/while/body/eval_jaxpr/ppermute | solution.py:11
  450.2 30.1 %collective-permute-start = (bf16[128,512]{1,0:T(8,128)(2,1)S(1)}, bf16[128,512]{1,0:T(8,128)(2,1)S(1)}, u32[]{:S(2)}, u32[]{:S(2)}) collective-permute-start(bf16[128,512]{1,0:T(8,128)(2,1)S(1)} %get-tuple-element.784), channel_id=1, source_target_pairs={{504,0},{0,8},{8,16},{16,24},{24,32},{32,40},{40,48},{48,56},{56,6... | collective-permute-start | bytes 393224 | tf_op jit(solution)/shard_map/while/body/eval_jaxpr/ppermute | solution.py:11
  496.9 38.1 %collective-permute-start = (bf16[128,512]{1,0:T(8,128)(2,1)S(1)}, bf16[128,512]{1,0:T(8,128)(2,1)S(1)}, u32[]{:S(2)}, u32[]{:S(2)}) collective-permute-start(bf16[128,512]{1,0:T(8,128)(2,1)S(1)} %get-tuple-element.784), channel_id=1, source_target_pairs={{504,0},{0,8},{8,16},{16,24},{24,32},{32,40},{40,48},{48,56},{56,6... | collective-permute-start | bytes 393224 | tf_op jit(solution)/shard_map/while/body/eval_jaxpr/ppermute | solution.py:11
  606.8 52.8 %collective-permute-start = (bf16[128,512]{1,0:T(8,128)(2,1)S(1)}, bf16[128,512]{1,0:T(8,128)(2,1)S(1)}, u32[]{:S(2)}, u32[]{:S(2)}) collective-permute-start(bf16[128,512]{1,0:T(8,128)(2,1)S(1)} %get-tuple-element.784), channel_id=1, source_target_pairs={{504,0},{0,8},{8,16},{16,24},{24,32},{32,40},{40,48},{48,56},{56,6... | collective-permute-start | bytes 393224 | tf_op jit(solution)/shard_map/while/body/eval_jaxpr/ppermute | solution.py:11
  699.5 54.0 %collective-permute-start = (bf16[128,512]{1,0:T(8,128)(2,1)S(1)}, bf16[128,512]{1,0:T(8,128)(2,1)S(1)}, u32[]{:S(2)}, u32[]{:S(2)}) collective-permute-start(bf16[128,512]{1,0:T(8,128)(2,1)S(1)} %get-tuple-element.784), channel_id=1, source_target_pairs={{504,0},{0,8},{8,16},{16,24},{24,32},{32,40},{40,48},{48,56},{56,6... | collective-permute-start | bytes 393224 | tf_op jit(solution)/shard_map/while/body/eval_jaxpr/ppermute | solution.py:11
  791.0 31.5 %collective-permute-start = (bf16[128,512]{1,0:T(8,128)(2,1)S(1)}, bf16[128,512]{1,0:T(8,128)(2,1)S(1)}, u32[]{:S(2)}, u32[]{:S(2)}) collective-permute-start(bf16[128,512]{1,0:T(8,128)(2,1)S(1)} %get-tuple-element.784), channel_id=1, source_target_pairs={{504,0},{0,8},{8,16},{16,24},{24,32},{32,40},{40,48},{48,56},{56,6... | collective-permute-start | bytes 393224 | tf_op jit(solution)/shard_map/while/body/eval_jaxpr/ppermute | solution.py:11
  833.9 36.9 %collective-permute-start = (bf16[128,512]{1,0:T(8,128)(2,1)S(1)}, bf16[128,512]{1,0:T(8,128)(2,1)S(1)}, u32[]{:S(2)}, u32[]{:S(2)}) collective-permute-start(bf16[128,512]{1,0:T(8,128)(2,1)S(1)} %get-tuple-element.784), channel_id=1, source_target_pairs={{504,0},{0,8},{8,16},{16,24},{24,32},{32,40},{40,48},{48,56},{56,6... | collective-permute-start | bytes 393224 | tf_op jit(solution)/shard_map/while/body/eval_jaxpr/ppermute | solution.py:11
  872.0 22.3 %collective-permute-start = (bf16[128,512]{1,0:T(8,128)(2,1)S(1)}, bf16[128,512]{1,0:T(8,128)(2,1)S(1)}, u32[]{:S(2)}, u32[]{:S(2)}) collective-permute-start(bf16[128,512]{1,0:T(8,128)(2,1)S(1)} %get-tuple-element.784), channel_id=1, source_target_pairs={{504,0},{0,8},{8,16},{16,24},{24,32},{32,40},{40,48},{48,56},{56,6... | collective-permute-start | bytes 393224 | tf_op jit(solution)/shard_map/while/body/eval_jaxpr/ppermute | solution.py:11
  895.5 47.5 %collective-permute-start = (bf16[128,512]{1,0:T(8,128)(2,1)S(1)}, bf16[128,512]{1,0:T(8,128)(2,1)S(1)}, u32[]{:S(2)}, u32[]{:S(2)}) collective-permute-start(bf16[128,512]{1,0:T(8,128)(2,1)S(1)} %get-tuple-element.784), channel_id=1, source_target_pairs={{504,0},{0,8},{8,16},{16,24},{24,32},{32,40},{40,48},{48,56},{56,6... | collective-permute-start | bytes 393224 | tf_op jit(solution)/shard_map/while/body/eval_jaxpr/ppermute | solution.py:11
  944.1 22.2 %collective-permute-start = (bf16[128,512]{1,0:T(8,128)(2,1)S(1)}, bf16[128,512]{1,0:T(8,128)(2,1)S(1)}, u32[]{:S(2)}, u32[]{:S(2)}) collective-permute-start(bf16[128,512]{1,0:T(8,128)(2,1)S(1)} %get-tuple-element.784), channel_id=1, source_target_pairs={{504,0},{0,8},{8,16},{16,24},{24,32},{32,40},{40,48},{48,56},{56,6... | collective-permute-start | bytes 393224 | tf_op jit(solution)/shard_map/while/body/eval_jaxpr/ppermute | solution.py:11
  1096.2 27.7 %collective-permute-start = (bf16[128,512]{1,0:T(8,128)(2,1)S(1)}, bf16[128,512]{1,0:T(8,128)(2,1)S(1)}, u32[]{:S(2)}, u32[]{:S(2)}) collective-permute-start(bf16[128,512]{1,0:T(8,128)(2,1)S(1)} %get-tuple-element.784), channel_id=1, source_target_pairs={{504,0},{0,8},{8,16},{16,24},{24,32},{32,40},{40,48},{48,56},{56,6... | collective-permute-start | bytes 393224 | tf_op jit(solution)/shard_map/while/body/eval_jaxpr/ppermute | solution.py:11
  1175.8 67.5 %collective-permute-start = (bf16[128,512]{1,0:T(8,128)(2,1)S(1)}, bf16[128,512]{1,0:T(8,128)(2,1)S(1)}, u32[]{:S(2)}, u32[]{:S(2)}) collective-permute-start(bf16[128,512]{1,0:T(8,128)(2,1)S(1)} %get-tuple-element.784), channel_id=1, source_target_pairs={{504,0},{0,8},{8,16},{16,24},{24,32},{32,40},{40,48},{48,56},{56,6... | collective-permute-start | bytes 393224 | tf_op jit(solution)/shard_map/while/body/eval_jaxpr/ppermute | solution.py:11
  1355.9 24.2 %collective-permute-start = (bf16[128,512]{1,0:T(8,128)(2,1)S(1)}, bf16[128,512]{1,0:T(8,128)(2,1)S(1)}, u32[]{:S(2)}, u32[]{:S(2)}) collective-permute-start(bf16[128,512]{1,0:T(8,128)(2,1)S(1)} %get-tuple-element.784), channel_id=1, source_target_pairs={{504,0},{0,8},{8,16},{16,24},{24,32},{32,40},{40,48},{48,56},{56,6... | collective-permute-start | bytes 393224 | tf_op jit(solution)/shard_map/while/body/eval_jaxpr/ppermute | solution.py:11
  1381.3 35.7 %collective-permute-start = (bf16[128,512]{1,0:T(8,128)(2,1)S(1)}, bf16[128,512]{1,0:T(8,128)(2,1)S(1)}, u32[]{:S(2)}, u32[]{:S(2)}) collective-permute-start(bf16[128,512]{1,0:T(8,128)(2,1)S(1)} %get-tuple-element.784), channel_id=1, source_target_pairs={{504,0},{0,8},{8,16},{16,24},{24,32},{32,40},{40,48},{48,56},{56,6... | collective-permute-start | bytes 393224 | tf_op jit(solution)/shard_map/while/body/eval_jaxpr/ppermute | solution.py:11
  1426.1 34.1 %collective-permute-start = (bf16[128,512]{1,0:T(8,128)(2,1)S(1)}, bf16[128,512]{1,0:T(8,128)(2,1)S(1)}, u32[]{:S(2)}, u32[]{:S(2)}) collective-permute-start(bf16[128,512]{1,0:T(8,128)(2,1)S(1)} %get-tuple-element.784), channel_id=1, source_target_pairs={{504,0},{0,8},{8,16},{16,24},{24,32},{32,40},{40,48},{48,56},{56,6... | collective-permute-start | bytes 393224 | tf_op jit(solution)/shard_map/while/body/eval_jaxpr/ppermute | solution.py:11
  1469.2 42.0 %collective-permute-start = (bf16[128,512]{1,0:T(8,128)(2,1)S(1)}, bf16[128,512]{1,0:T(8,128)(2,1)S(1)}, u32[]{:S(2)}, u32[]{:S(2)}) collective-permute-start(bf16[128,512]{1,0:T(8,128)(2,1)S(1)} %get-tuple-element.784), channel_id=1, source_target_pairs={{504,0},{0,8},{8,16},{16,24},{24,32},{32,40},{40,48},{48,56},{56,6... | collective-permute-start | bytes 393224 | tf_op jit(solution)/shard_map/while/body/eval_jaxpr/ppermute | solution.py:11
  1553.4 42.4 %collective-permute-start = (bf16[128,512]{1,0:T(8,128)(2,1)S(1)}, bf16[128,512]{1,0:T(8,128)(2,1)S(1)}, u32[]{:S(2)}, u32[]{:S(2)}) collective-permute-start(bf16[128,512]{1,0:T(8,128)(2,1)S(1)} %get-tuple-element.784), channel_id=1, source_target_pairs={{504,0},{0,8},{8,16},{16,24},{24,32},{32,40},{40,48},{48,56},{56,6... | collective-permute-start | bytes 393224 | tf_op jit(solution)/shard_map/while/body/eval_jaxpr/ppermute | solution.py:11
  1604.9 38.1 %collective-permute-start = (bf16[128,512]{1,0:T(8,128)(2,1)S(1)}, bf16[128,512]{1,0:T(8,128)(2,1)S(1)}, u32[]{:S(2)}, u32[]{:S(2)}) collective-permute-start(bf16[128,512]{1,0:T(8,128)(2,1)S(1)} %get-tuple-element.784), channel_id=1, source_target_pairs={{504,0},{0,8},{8,16},{16,24},{24,32},{32,40},{40,48},{48,56},{56,6... | collective-permute-start | bytes 393224 | tf_op jit(solution)/shard_map/while/body/eval_jaxpr/ppermute | solution.py:11
  (47 other events, 831.6 us)
Sparse Core Ops, SparseCore 0:
  1684.5 208.3 reduce-scatter.1
